TPU v7x, 32 devices: a whole 2x2x4 slice. The times are simulated.
32 devices in a mesh: region: 8 (over y, x, core), cuts: 4 (over z).
Axes of the slice: x: 2, y: 2, z: 4, core: 2. Of those that a mesh axis runs over, the one named last changes fastest.
Arguments:
- history: bfloat16 [8, 8192, 128], P(None, ('region', 'cuts')), may hold values from -6 to 6
- incident: bfloat16 [4, 8192, 128], P(None, ('region', 'cuts')), may hold values from -6 to 6
- self_inverse: bfloat16 [8192, 256], P(('region', 'cuts')), may hold values from -0.375 to 0.375
- lag_kernels: bfloat16 [384, 8, 256, 256], P(('region', 'cuts')), may hold values from -0.02734375 to 0.02734375
- pair_partner: int32 [384], P(('region', 'cuts')), may hold values from 0 to 11
- pair_lags: int32 [384], P(('region', 'cuts')), may hold values from 1 to 8
Outputs:
- densities: bfloat16 [4, 8192, 128], P(None, ('region', 'cuts'))
Inputs may be any that keep to these rules, and one draw needn't show every extreme that they name: `pair_partner`: codes below 4 name a block of the region before the owner's, codes from 8 on one of the region after it, the others one of the owner's region; the same block may be named by several pairs, and a pair's partner may be its owner. Pair p uses lag matrices 1 to pair_lags[p]; the rest are stored but unused.
All inputs are finite; a program needn't handle non-finite values.
Results may differ from a plain program's by a relative error of at most 0.0095.
Values may be sent and summed in bfloat16 or wider, within the bound.
No kernel may reach another device: no remote copies, remote signals or barrier semaphores. Data moves between devices by JAX's collectives and lax.ppermute only.
A program may use at most 128 MiB of HBM per device.

v0:
```python
import jax
import jax.numpy as jnp
from jax import lax
from jax.sharding import PartitionSpec as P


def padded(block, sides, width):
    for axis, dim in sides:
        count = lax.axis_size(axis)
        forward = [(i, i + 1) for i in range(count - 1)]
        forward.append((count - 1, 0))
        backward = [(target, source) for source, target in forward]
        low = lax.ppermute(
            lax.slice_in_dim(block, block.shape[dim] - width, None, axis=dim), axis, forward
        )
        high = lax.ppermute(lax.slice_in_dim(block, 0, width, axis=dim), axis, backward)
        block = jnp.concatenate([low, block, high], axis=dim)
    return block


def shifted(block, axis, distance):
    devices = range(lax.axis_size(axis))
    route = [((i - distance) % len(devices), i) for i in devices]
    return lax.ppermute(block, axis, route)


def lag_gate(pair_lags, lag_total):
    lag_ids = lax.iota(jnp.int32, lag_total) + 1
    return (lag_ids[None, :] <= pair_lags[:, None]).astype(jnp.bfloat16)


def near_field(lag_kernels, window, recent, pair_partner, gate_table, cut_count, own_cut):
    partner_hist = jnp.take(window, pair_partner, axis=1)
    partner_hist = partner_hist * jnp.transpose(gate_table)[:, :, None, None]
    forward = jnp.einsum(
        "plij,lpjr->ir", lag_kernels, partner_hist, preferred_element_type=jnp.float32
    )
    own_hist = gate_table[:, :, None, None] * recent[None]
    backward = jnp.einsum(
        "plij,plir->pjr", lag_kernels, own_hist, preferred_element_type=jnp.float32
    )
    slot_codes = lax.iota(jnp.int32, 3 * cut_count)
    select = (slot_codes[:, None] == pair_partner[None, :]).astype(jnp.float32)
    spread = jnp.einsum("qp,pjr->qjr", select, backward, precision=lax.Precision.HIGHEST)
    own_slot = (slot_codes == cut_count + own_cut).astype(jnp.float32)
    return spread + own_slot[:, None, None] * forward[None]


def on_device(history, incident, self_inverse, lag_kernels, pair_partner, pair_lags):
    lag_total = history.shape[0]
    step_total = incident.shape[0]
    panel_count = history.shape[1]
    column_count = history.shape[2]
    cut_count = lax.axis_size("cuts")
    own_cut = lax.axis_index("cuts")
    gate_table = lag_gate(pair_lags, lag_total)
    recent = history
    window = history
    outputs = []
    for step_now in range(step_total):
        stacked = lax.all_gather(recent[:, None, None], "cuts", axis=2, tiled=True)
        bordered = padded(stacked, (("region", 1),), 1)
        window = bordered.reshape(lag_total, 3 * cut_count, panel_count, column_count)
        partial_field = near_field(
            lag_kernels, window, recent, pair_partner, gate_table, cut_count, own_cut
        )
        grouped = partial_field.reshape(3, cut_count, panel_count, column_count)
        from_above = shifted(grouped[0].astype(jnp.bfloat16), "region", -1).astype(jnp.float32)
        from_below = shifted(grouped[2].astype(jnp.bfloat16), "region", 1).astype(jnp.float32)
        field_sum = lax.psum_scatter(
            grouped[1] + from_above + from_below, "cuts", scatter_dimension=0, tiled=True
        )[0]
        excess = (incident[step_now].astype(jnp.float32) - field_sum).astype(jnp.bfloat16)
        density = jnp.dot(self_inverse, excess, preferred_element_type=jnp.float32).astype(
            jnp.bfloat16
        )
        outputs.append(density)
        recent = jnp.concatenate([density[None], recent[:-1]], axis=0)
    return jnp.stack(outputs)


def solution(mesh):
    return jax.shard_map(
        on_device,
        mesh=mesh,
        in_specs=(
            P(None, ("region", "cuts"), None),
            P(None, ("region", "cuts"), None),
            P(("region", "cuts"), None),
            P(("region", "cuts"), None, None, None),
            P(("region", "cuts")),
            P(("region", "cuts")),
        ),
        out_specs=P(None, ("region", "cuts"), None),
        check_vma=False,
    )
```

profile of v0, /device:TPU:0, one launch (start us, length us, event | category | flops | bytes accessed | tf_op | source)
XLA Modules:
  0.0 628.3 jit_solution(11969034751456141057)
XLA Ops:
  9.3 48.0 %all-gather.9.cloned.1.call-done = bf16[8,1024,128]{2,1,0:T(8,128)(2,1)} async-done(((bf16[8,256,128]{2,1,0:T(8,128)(2,1)}), bf16[8,1024,128]{2,1,0:T(8,128)(2,1)}) %all-gather.9.cloned.1.call-update) | async-done | bytes 2097168 | tf_op jit(solution)/shard_map/all_gather | solution.py:61
  57.3 1.7 collective-permute-start.1
  59.0 7.6 %fusion.28 = f32[12,256,128]{1,2,0:T(8,128)} fusion(bf16[12,8,256,256]{3,2,1,0:T(8,128)(2,1)} %param.11, bf16[8,256,128]{1,2,0:T(8,128)(2,1)S(1)} %copy.43, bf16[12,8]{1,0:T(8,128)(2,1)S(1)} %compare_convert_fusion.1), kind=kOutput, calls=%fused_computation.44 | convolution fusion | flops 1613758464 | bytes 14680256 | tf_op jit(solution)/shard_map/plij,plir->pjr/dot_general | solution.py:39
  66.6 2.1 copy.44
  68.9 35.7 %collective-permute-done.1 = bf16[8,1,4,256,128]{4,3,2,1,0:T(8,128)(2,1)} collective-permute-done((bf16[8,1,4,256,128]{4,3,2,1,0:T(8,128)(2,1)}, bf16[8,1,4,256,128]{4,3,2,1,0:T(8,128)(2,1)}, u32[]{:S(2)}, u32[]{:S(2)}) %collective-permute-start.1) | collective-permute-done | bytes 2097184 | tf_op jit(solution)/shard_map/ppermute | solution.py:16
  104.6 1.9 collective-permute-done
  106.5 6.5 %pad_maximum_fusion = bf16[8,3,4,256,128]{4,3,2,1,0:T(8,128)(2,1)} fusion(bf16[8,1,4,256,128]{4,3,2,1,0:T(8,128)(2,1)} %collective-permute-done.1, bf16[8,1,4,256,128]{4,3,2,1,0:T(8,128)(2,1)} %bitcast.128, bf16[8,1,4,256,128]{4,3,2,1,0:T(8,128)(2,1)} %collective-permute-done), kind=kLoop, calls=%fused_computation.12 | loop fusion | flops 6291456 | bytes 12582912 | tf_op jit(solution)/shard_map/concatenate | solution.py:17
  113.0 6.9 %gather_fusion = bf16[12,8,256,128]{3,2,1,0:T(8,128)(2,1)} fusion(bf16[8,12,256,128]{3,2,1,0:T(8,128)(2,1)} %bitcast.123, s32[1024]{0:T(1024)S(1)} %pad_clamp_fusion), kind=kCustom, calls=%fused_computation.clone | custom fusion | bytes 12582960 | tf_op jit(solution)/shard_map/jit(_take)/gather | solution.py:33
  119.9 12.1 %fusion.40 = f32[256,128]{0,1:T(8,128)S(1)} fusion(bf16[12,8,256,256]{3,2,1,0:T(8,128)(2,1)} %param.11, bf16[12,8,256,128]{3,2,1,0:T(8,128)(2,1)} %gather_fusion, pred[12]{0:T(512)(128)(4,1)S(1)} %compare_and_fusion, bf16[8,12]{0,1:T(8,128)(2,1)S(1)} %compare_convert_fusion), kind=kOutput, calls=%fused_computation.48 | convolution fusion | flops 1616904192 | bytes 19005644 | tf_op jit(solution)/shard_map/plij,lpjr->ir/dot_general | solution.py:35
  133.7 2.6 collective-permute-start.2
  136.3 6.1 collective-permute-done.3
  143.6 19.7 %reduce-scatter.5.cloned.1.call-done = f32[1,256,128]{2,1,0:T(8,128)} async-done(((f32[4,256,128]{2,1,0:T(8,128)}), f32[1,256,128]{2,1,0:T(8,128)}) %reduce-scatter.5.cloned.1.call-update) | async-done | bytes 131088 | tf_op jit(solution)/shard_map/reduce_scatter | solution.py:70
  165.5 44.0 %all-gather.11.cloned.1.call-done = bf16[8,1024,128]{2,1,0:T(8,128)(2,1)} async-done(((bf16[8,256,128]{2,1,0:T(8,128)(2,1)}), bf16[8,1024,128]{2,1,0:T(8,128)(2,1)}) %all-gather.11.cloned.1.call-update) | async-done | bytes 2097168 | tf_op jit(solution)/shard_map/all_gather | solution.py:61
  209.5 1.7 collective-permute-start.5
  212.9 7.6 %fusion.31 = f32[12,256,128]{1,2,0:T(8,128)} fusion(bf16[12,8,256,256]{3,2,1,0:T(8,128)(2,1)} %param.11, bf16[8,256,128]{1,2,0:T(8,128)(2,1)S(1)} %copy.50, bf16[12,8]{1,0:T(8,128)(2,1)S(1)} %compare_convert_fusion.1), kind=kOutput, calls=%fused_computation.45 | convolution fusion | flops 1613758464 | bytes 14680256 | tf_op jit(solution)/shard_map/plij,plir->pjr/dot_general | solution.py:39
  220.5 2.1 copy.51
  222.6 34.6 %collective-permute-done.5 = bf16[8,1,4,256,128]{4,3,2,1,0:T(8,128)(2,1)} collective-permute-done((bf16[8,1,4,256,128]{4,3,2,1,0:T(8,128)(2,1)}, bf16[8,1,4,256,128]{4,3,2,1,0:T(8,128)(2,1)}, u32[]{:S(2)}, u32[]{:S(2)}) %collective-permute-start.5) | collective-permute-done | bytes 2097184 | tf_op jit(solution)/shard_map/ppermute | solution.py:16
  257.2 1.5 collective-permute-done.4
  258.7 6.5 %pad_maximum_fusion.1 = bf16[8,3,4,256,128]{4,3,2,1,0:T(8,128)(2,1)} fusion(bf16[8,1,4,256,128]{4,3,2,1,0:T(8,128)(2,1)} %collective-permute-done.5, bf16[8,1,4,256,128]{4,3,2,1,0:T(8,128)(2,1)} %bitcast.134, bf16[8,1,4,256,128]{4,3,2,1,0:T(8,128)(2,1)} %collective-permute-done.4), kind=kLoop, calls=%fused_computation.13 | loop fusion | flops 6291456 | bytes 12582912 | tf_op jit(solution)/shard_map/concatenate | solution.py:17
  265.1 6.9 %gather_fusion.1 = bf16[12,8,256,128]{3,2,1,0:T(8,128)(2,1)} fusion(bf16[8,12,256,128]{3,2,1,0:T(8,128)(2,1)} %bitcast.124, s32[1024]{0:T(1024)S(1)} %pad_clamp_fusion), kind=kCustom, calls=%fused_computation.1.clone | custom fusion | bytes 12582960 | tf_op jit(solution)/shard_map/jit(_take)/gather | solution.py:33
  272.1 12.1 %fusion.45 = f32[256,128]{0,1:T(8,128)S(1)} fusion(bf16[12,8,256,256]{3,2,1,0:T(8,128)(2,1)} %param.11, bf16[12,8,256,128]{3,2,1,0:T(8,128)(2,1)} %gather_fusion.1, pred[12]{0:T(512)(128)(4,1)S(1)} %copy-done.9, bf16[8,12]{0,1:T(8,128)(2,1)S(1)} %copy-done.5), kind=kOutput, calls=%fused_computation.49 | convolution fusion | flops 1616904192 | bytes 19005644 | tf_op jit(solution)/shard_map/plij,lpjr->ir/dot_general | solution.py:35
  285.8 2.6 collective-permute-start.6
  288.5 6.1 collective-permute-done.7
  295.8 19.6 %reduce-scatter.7.cloned.1.call-done = f32[1,256,128]{2,1,0:T(8,128)} async-done(((f32[4,256,128]{2,1,0:T(8,128)}), f32[1,256,128]{2,1,0:T(8,128)}) %reduce-scatter.7.cloned.1.call-update) | async-done | bytes 131088 | tf_op jit(solution)/shard_map/reduce_scatter | solution.py:70
  317.6 44.0 %all-gather.13.cloned.1.call-done = bf16[8,1024,128]{2,1,0:T(8,128)(2,1)} async-done(((bf16[8,256,128]{2,1,0:T(8,128)(2,1)}), bf16[8,1024,128]{2,1,0:T(8,128)(2,1)}) %all-gather.13.cloned.1.call-update) | async-done | bytes 2097168 | tf_op jit(solution)/shard_map/all_gather | solution.py:61
  361.6 1.7 collective-permute-start.9
  364.7 7.6 %fusion.34 = f32[12,256,128]{1,2,0:T(8,128)} fusion(bf16[12,8,256,256]{3,2,1,0:T(8,128)(2,1)} %param.11, bf16[8,256,128]{1,2,0:T(8,128)(2,1)S(1)} %copy.57, bf16[12,8]{1,0:T(8,128)(2,1)S(1)} %compare_convert_fusion.1), kind=kOutput, calls=%fused_computation.46 | convolution fusion | flops 1613758464 | bytes 14680256 | tf_op jit(solution)/shard_map/plij,plir->pjr/dot_general | solution.py:39
  372.3 2.1 copy.58
  374.5 34.6 %collective-permute-done.9 = bf16[8,1,4,256,128]{4,3,2,1,0:T(8,128)(2,1)} collective-permute-done((bf16[8,1,4,256,128]{4,3,2,1,0:T(8,128)(2,1)}, bf16[8,1,4,256,128]{4,3,2,1,0:T(8,128)(2,1)}, u32[]{:S(2)}, u32[]{:S(2)}) %collective-permute-start.9) | collective-permute-done | bytes 2097184 | tf_op jit(solution)/shard_map/ppermute | solution.py:16
  409.0 1.8 collective-permute-done.8
  410.8 6.5 %pad_maximum_fusion.2 = bf16[8,3,4,256,128]{4,3,2,1,0:T(8,128)(2,1)} fusion(bf16[8,1,4,256,128]{4,3,2,1,0:T(8,128)(2,1)} %collective-permute-done.9, bf16[8,1,4,256,128]{4,3,2,1,0:T(8,128)(2,1)} %bitcast.137, bf16[8,1,4,256,128]{4,3,2,1,0:T(8,128)(2,1)} %collective-permute-done.8), kind=kLoop, calls=%fused_computation.14 | loop fusion | flops 6291456 | bytes 12582912 | tf_op jit(solution)/shard_map/concatenate | solution.py:17
  417.3 6.9 %gather_fusion.2 = bf16[12,8,256,128]{3,2,1,0:T(8,128)(2,1)} fusion(bf16[8,12,256,128]{3,2,1,0:T(8,128)(2,1)} %bitcast.125, s32[1024]{0:T(1024)S(1)} %pad_clamp_fusion), kind=kCustom, calls=%fused_computation.2.clone | custom fusion | bytes 12582960 | tf_op jit(solution)/shard_map/jit(_take)/gather | solution.py:33
  424.2 12.1 %fusion.50 = f32[256,128]{0,1:T(8,128)S(1)} fusion(bf16[12,8,256,256]{3,2,1,0:T(8,128)(2,1)} %param.11, bf16[12,8,256,128]{3,2,1,0:T(8,128)(2,1)} %gather_fusion.2, pred[12]{0:T(512)(128)(4,1)S(1)} %copy-done.10, bf16[8,12]{0,1:T(8,128)(2,1)S(1)} %copy-done.6), kind=kOutput, calls=%fused_computation.50 | convolution fusion | flops 1616904192 | bytes 19005644 | tf_op jit(solution)/shard_map/plij,lpjr->ir/dot_general | solution.py:35
  438.0 2.6 collective-permute-start.10
  440.6 6.1 collective-permute-done.11
  447.9 19.5 %reduce-scatter.9.cloned.1.call-done = f32[1,256,128]{2,1,0:T(8,128)} async-done(((f32[4,256,128]{2,1,0:T(8,128)}), f32[1,256,128]{2,1,0:T(8,128)}) %reduce-scatter.9.cloned.1.call-update) | async-done | bytes 131088 | tf_op jit(solution)/shard_map/reduce_scatter | solution.py:70
  469.6 44.0 %all-gather.15.cloned.1.call-done = bf16[8,1024,128]{2,1,0:T(8,128)(2,1)} async-done(((bf16[8,256,128]{2,1,0:T(8,128)(2,1)}), bf16[8,1024,128]{2,1,0:T(8,128)(2,1)}) %all-gather.15.cloned.1.call-update) | async-done | bytes 2097168 | tf_op jit(solution)/shard_map/all_gather | solution.py:61
  513.6 1.7 collective-permute-start.13
  516.7 7.6 %fusion.37 = f32[12,256,128]{1,2,0:T(8,128)} fusion(bf16[12,8,256,256]{3,2,1,0:T(8,128)(2,1)} %param.11, bf16[8,256,128]{1,2,0:T(8,128)(2,1)S(1)} %copy.64, bf16[12,8]{1,0:T(8,128)(2,1)S(1)} %compare_convert_fusion.1), kind=kOutput, calls=%fused_computation.47 | convolution fusion | flops 1613758464 | bytes 14680256 | tf_op jit(solution)/shard_map/plij,plir->pjr/dot_general | solution.py:39
  524.3 2.1 copy.65
  526.4 34.6 %collective-permute-done.13 = bf16[8,1,4,256,128]{4,3,2,1,0:T(8,128)(2,1)} collective-permute-done((bf16[8,1,4,256,128]{4,3,2,1,0:T(8,128)(2,1)}, bf16[8,1,4,256,128]{4,3,2,1,0:T(8,128)(2,1)}, u32[]{:S(2)}, u32[]{:S(2)}) %collective-permute-start.13) | collective-permute-done | bytes 2097184 | tf_op jit(solution)/shard_map/ppermute | solution.py:16
  561.0 1.7 collective-permute-done.12
  562.7 6.5 %pad_maximum_fusion.3 = bf16[8,3,4,256,128]{4,3,2,1,0:T(8,128)(2,1)} fusion(bf16[8,1,4,256,128]{4,3,2,1,0:T(8,128)(2,1)} %collective-permute-done.13, bf16[8,1,4,256,128]{4,3,2,1,0:T(8,128)(2,1)} %bitcast.131, bf16[8,1,4,256,128]{4,3,2,1,0:T(8,128)(2,1)} %collective-permute-done.12), kind=kLoop, calls=%fused_computation.15 | loop fusion | flops 6291456 | bytes 12582912 | tf_op jit(solution)/shard_map/concatenate | solution.py:17
  569.2 6.9 %gather_fusion.3 = bf16[12,8,256,128]{3,2,1,0:T(8,128)(2,1)} fusion(bf16[8,12,256,128]{3,2,1,0:T(8,128)(2,1)} %bitcast.122, s32[1024]{0:T(1024)S(1)} %pad_clamp_fusion), kind=kCustom, calls=%fused_computation.3.clone | custom fusion | bytes 12582960 | tf_op jit(solution)/shard_map/jit(_take)/gather | solution.py:33
  576.1 12.1 %fusion.55 = f32[256,128]{0,1:T(8,128)S(1)} fusion(bf16[12,8,256,256]{3,2,1,0:T(8,128)(2,1)} %param.11, bf16[12,8,256,128]{3,2,1,0:T(8,128)(2,1)} %gather_fusion.3, pred[12]{0:T(512)(128)(4,1)S(1)} %copy-done.10, bf16[8,12]{0,1:T(8,128)(2,1)S(1)} %copy-done.6), kind=kOutput, calls=%fused_computation.51 | convolution fusion | flops 1616904192 | bytes 19005644 | tf_op jit(solution)/shard_map/plij,lpjr->ir/dot_general | solution.py:35
  589.9 2.6 collective-permute-start.14
  592.5 6.1 collective-permute-done.15
  599.7 19.5 %reduce-scatter.11.cloned.1.call-done = f32[1,256,128]{2,1,0:T(8,128)} async-done(((f32[4,256,128]{2,1,0:T(8,128)}), f32[1,256,128]{2,1,0:T(8,128)}) %reduce-scatter.11.cloned.1.call-update) | async-done | bytes 131088 | tf_op jit(solution)/shard_map/reduce_scatter | solution.py:70
  (96 shorter events, 26.9 us)
Async XLA Ops:
  6.5 156.8 %copy-start = (bf16[256,256]{1,0:T(8,128)(2,1)S(1)}, bf16[256,256]{1,0:T(8,128)(2,1)}, u32[]{:S(2)}) copy-start(bf16[256,256]{1,0:T(8,128)(2,1)} %param.10) | copy-start | bytes 393220
  6.5 50.8 %all-gather.9.cloned.1.call-start = ((), (), s32[]{:S(2)}) async-start(), calls=%async_computation.8 | async-start | bytes 2621440 | tf_op jit(solution)/shard_map/all_gather | solution.py:61
  7.3 156.1 %reduce-scatter.5.cloned.1.call-start = ((), (), s32[]{:S(2)}) async-start(), calls=%async_computation.4 | async-start | bytes 655360 | tf_op jit(solution)/shard_map/reduce_scatter | solution.py:70
  57.3 11.4 %copy-start.3 = (s32[12]{0:T(128)S(1)}, s32[12]{0:T(128)}, u32[]{:S(2)}) copy-start(s32[12]{0:T(128)} %param.12) | copy-start | bytes 148
  57.3 11.5 %copy-start.7 = (s32[12]{0:T(128)S(1)}, s32[12]{0:T(128)}, u32[]{:S(2)}) copy-start(s32[12]{0:T(128)} %param.13) | copy-start | bytes 148
  57.3 47.2 %collective-permute-start.1 = (bf16[8,1,4,256,128]{4,3,2,1,0:T(8,128)(2,1)}, bf16[8,1,4,256,128]{4,3,2,1,0:T(8,128)(2,1)}, u32[]{:S(2)}, u32[]{:S(2)}) collective-permute-start(bf16[8,1,4,256,128]{4,3,2,1,0:T(8,128)(2,1)} %bitcast.126), channel_id=1, source_target_pairs={{4,0},{8,4},{12,8},{16,12},{20,16},{24,20},{28,24},{0,28},{5,1},{9... | collective-permute-start | bytes 6291464 | tf_op jit(solution)/shard_map/ppermute | solution.py:16
  59.0 47.5 %collective-permute-start = (bf16[8,1,4,256,128]{4,3,2,1,0:T(8,128)(2,1)}, bf16[8,1,4,256,128]{4,3,2,1,0:T(8,128)(2,1)}, u32[]{:S(2)}, u32[]{:S(2)}) collective-permute-start(bf16[8,1,4,256,128]{4,3,2,1,0:T(8,128)(2,1)} %bitcast.127), channel_id=1, source_target_pairs={{0,4},{4,8},{8,12},{12,16},{16,20},{20,24},{24,28},{28,0},{1,5},{5... | collective-permute-start | bytes 6291464 | tf_op jit(solution)/shard_map/ppermute | solution.py:13
  68.8 51.1 %copy-start.8 = (pred[12]{0:T(512)(128)(4,1)}, pred[12]{0:T(512)(128)(4,1)S(1)}, u32[]{:S(2)}) copy-start(pred[12]{0:T(512)(128)(4,1)S(1)} %compare_and_fusion) | copy-start | bytes 40
  68.9 51.0 %copy-start.4 = (bf16[8,12]{0,1:T(8,128)(2,1)}, bf16[8,12]{0,1:T(8,128)(2,1)S(1)}, u32[]{:S(2)}) copy-start(bf16[8,12]{0,1:T(8,128)(2,1)S(1)} %compare_convert_fusion) | copy-start | bytes 580
  132.0 11.6 %copy-start.1 = (bf16[8,256,128]{2,1,0:T(8,128)(2,1)S(1)}, bf16[8,256,128]{2,1,0:T(8,128)(2,1)}, u32[]{:S(2)}) copy-start(bf16[8,256,128]{2,1,0:T(8,128)(2,1)} %param.8) | copy-start | bytes 1572868
  132.0 31.4 %copy-start.2 = (bf16[4,256,128]{2,1,0:T(8,128)(2,1)S(1)}, bf16[4,256,128]{2,1,0:T(8,128)(2,1)}, u32[]{:S(2)}) copy-start(bf16[4,256,128]{2,1,0:T(8,128)(2,1)} %param.9) | copy-start | bytes 786436
  133.6 8.8 %collective-permute-start.3 = (bf16[4,256,128]{2,0,1:T(4,128)(2,1)S(1)}, bf16[4,256,128]{2,0,1:T(4,128)(2,1)S(1)}, u32[]{:S(2)}, u32[]{:S(2)}) collective-permute-start(bf16[4,256,128]{2,0,1:T(4,128)(2,1)S(1)} %get-tuple-element.13), channel_id=1, source_target_pairs={{28,0},{0,4},{4,8},{8,12},{12,16},{16,20},{20,24},{24,28},{29,1},{... | collective-permute-start | bytes 786440 | tf_op jit(solution)/shard_map/ppermute | solution.py:24
  133.7 8.8 %collective-permute-start.2 = (bf16[4,256,128]{2,0,1:T(4,128)(2,1)S(1)}, bf16[4,256,128]{2,0,1:T(4,128)(2,1)S(1)}, u32[]{:S(2)}, u32[]{:S(2)}) collective-permute-start(bf16[4,256,128]{2,0,1:T(4,128)(2,1)S(1)} %get-tuple-element.12), channel_id=1, source_target_pairs={{4,0},{8,4},{12,8},{16,12},{20,16},{24,20},{28,24},{0,28},{5,1},{9... | collective-permute-start | bytes 786440 | tf_op jit(solution)/shard_map/ppermute | solution.py:24
  143.5 66.0 %all-gather.11.cloned.1.call-start = ((), (), s32[]{:S(2)}) async-start(), calls=%async_computation.9 | async-start | bytes 2621440 | tf_op jit(solution)/shard_map/all_gather | solution.py:61
  165.5 150.0 %reduce-scatter.7.cloned.1.call-start = ((), (), s32[]{:S(2)}) async-start(), calls=%async_computation.5 | async-start | bytes 655360 | tf_op jit(solution)/shard_map/reduce_scatter | solution.py:70
  209.5 47.7 %collective-permute-start.5 = (bf16[8,1,4,256,128]{4,3,2,1,0:T(8,128)(2,1)}, bf16[8,1,4,256,128]{4,3,2,1,0:T(8,128)(2,1)}, u32[]{:S(2)}, u32[]{:S(2)}) collective-permute-start(bf16[8,1,4,256,128]{4,3,2,1,0:T(8,128)(2,1)} %bitcast.132), channel_id=1, source_target_pairs={{4,0},{8,4},{12,8},{16,12},{20,16},{24,20},{28,24},{0,28},{5,1},{9... | collective-permute-start | bytes 6291464 | tf_op jit(solution)/shard_map/ppermute | solution.py:16
  211.2 47.5 %collective-permute-start.4 = (bf16[8,1,4,256,128]{4,3,2,1,0:T(8,128)(2,1)}, bf16[8,1,4,256,128]{4,3,2,1,0:T(8,128)(2,1)}, u32[]{:S(2)}, u32[]{:S(2)}) collective-permute-start(bf16[8,1,4,256,128]{4,3,2,1,0:T(8,128)(2,1)} %bitcast.133), channel_id=1, source_target_pairs={{0,4},{4,8},{8,12},{12,16},{16,20},{20,24},{24,28},{28,0},{1,5},{5... | collective-permute-start | bytes 6291464 | tf_op jit(solution)/shard_map/ppermute | solution.py:13
  265.1 6.9 %copy-start.5 = (bf16[8,12]{0,1:T(8,128)(2,1)S(1)}, bf16[8,12]{0,1:T(8,128)(2,1)}, u32[]{:S(2)}) copy-start(bf16[8,12]{0,1:T(8,128)(2,1)} %copy-done.4) | copy-start | bytes 580
  265.1 6.9 %copy-start.9 = (pred[12]{0:T(512)(128)(4,1)S(1)}, pred[12]{0:T(512)(128)(4,1)}, u32[]{:S(2)}) copy-start(pred[12]{0:T(512)(128)(4,1)} %copy-done.8) | copy-start | bytes 40
  285.8 8.8 %collective-permute-start.7 = (bf16[4,256,128]{2,0,1:T(4,128)(2,1)S(1)}, bf16[4,256,128]{2,0,1:T(4,128)(2,1)S(1)}, u32[]{:S(2)}, u32[]{:S(2)}) collective-permute-start(bf16[4,256,128]{2,0,1:T(4,128)(2,1)S(1)} %get-tuple-element.11), channel_id=1, source_target_pairs={{28,0},{0,4},{4,8},{8,12},{12,16},{16,20},{20,24},{24,28},{29,1},{... | collective-permute-start | bytes 786440 | tf_op jit(solution)/shard_map/ppermute | solution.py:24
  285.8 8.8 %collective-permute-start.6 = (bf16[4,256,128]{2,0,1:T(4,128)(2,1)S(1)}, bf16[4,256,128]{2,0,1:T(4,128)(2,1)S(1)}, u32[]{:S(2)}, u32[]{:S(2)}) collective-permute-start(bf16[4,256,128]{2,0,1:T(4,128)(2,1)S(1)} %get-tuple-element.10), channel_id=1, source_target_pairs={{4,0},{8,4},{12,8},{16,12},{20,16},{24,20},{28,24},{0,28},{5,1},{9... | collective-permute-start | bytes 786440 | tf_op jit(solution)/shard_map/ppermute | solution.py:24
  295.7 65.9 %all-gather.13.cloned.1.call-start = ((), (), s32[]{:S(2)}) async-start(), calls=%async_computation.10 | async-start | bytes 2621440 | tf_op jit(solution)/shard_map/all_gather | solution.py:61
  317.6 149.9 %reduce-scatter.9.cloned.1.call-start = ((), (), s32[]{:S(2)}) async-start(), calls=%async_computation.6 | async-start | bytes 655360 | tf_op jit(solution)/shard_map/reduce_scatter | solution.py:70
  361.6 47.4 %collective-permute-start.9 = (bf16[8,1,4,256,128]{4,3,2,1,0:T(8,128)(2,1)}, bf16[8,1,4,256,128]{4,3,2,1,0:T(8,128)(2,1)}, u32[]{:S(2)}, u32[]{:S(2)}) collective-permute-start(bf16[8,1,4,256,128]{4,3,2,1,0:T(8,128)(2,1)} %bitcast.135), channel_id=1, source_target_pairs={{4,0},{8,4},{12,8},{16,12},{20,16},{24,20},{28,24},{0,28},{5,1},{9... | collective-permute-start | bytes 6291464 | tf_op jit(solution)/shard_map/ppermute | solution.py:16
  363.3 47.5 %collective-permute-start.8 = (bf16[8,1,4,256,128]{4,3,2,1,0:T(8,128)(2,1)}, bf16[8,1,4,256,128]{4,3,2,1,0:T(8,128)(2,1)}, u32[]{:S(2)}, u32[]{:S(2)}) collective-permute-start(bf16[8,1,4,256,128]{4,3,2,1,0:T(8,128)(2,1)} %bitcast.136), channel_id=1, source_target_pairs={{0,4},{4,8},{8,12},{12,16},{16,20},{20,24},{24,28},{28,0},{1,5},{5... | collective-permute-start | bytes 6291464 | tf_op jit(solution)/shard_map/ppermute | solution.py:13
  417.3 6.9 %copy-start.6 = (bf16[8,12]{0,1:T(8,128)(2,1)S(1)}, bf16[8,12]{0,1:T(8,128)(2,1)}, u32[]{:S(2)}) copy-start(bf16[8,12]{0,1:T(8,128)(2,1)} %copy-done.4) | copy-start | bytes 580
  417.3 6.9 %copy-start.10 = (pred[12]{0:T(512)(128)(4,1)S(1)}, pred[12]{0:T(512)(128)(4,1)}, u32[]{:S(2)}) copy-start(pred[12]{0:T(512)(128)(4,1)} %copy-done.8) | copy-start | bytes 40
  437.9 8.8 %collective-permute-start.11 = (bf16[4,256,128]{2,0,1:T(4,128)(2,1)S(1)}, bf16[4,256,128]{2,0,1:T(4,128)(2,1)S(1)}, u32[]{:S(2)}, u32[]{:S(2)}) collective-permute-start(bf16[4,256,128]{2,0,1:T(4,128)(2,1)S(1)} %get-tuple-element.9), channel_id=1, source_target_pairs={{28,0},{0,4},{4,8},{8,12},{12,16},{16,20},{20,24},{24,28},{29,1},{... | collective-permute-start | bytes 786440 | tf_op jit(solution)/shard_map/ppermute | solution.py:24
  438.0 8.8 %collective-permute-start.10 = (bf16[4,256,128]{2,0,1:T(4,128)(2,1)S(1)}, bf16[4,256,128]{2,0,1:T(4,128)(2,1)S(1)}, u32[]{:S(2)}, u32[]{:S(2)}) collective-permute-start(bf16[4,256,128]{2,0,1:T(4,128)(2,1)S(1)} %get-tuple-element.8), channel_id=1, source_target_pairs={{4,0},{8,4},{12,8},{16,12},{20,16},{24,20},{28,24},{0,28},{5,1},{9... | collective-permute-start | bytes 786440 | tf_op jit(solution)/shard_map/ppermute | solution.py:24
  447.8 65.7 %all-gather.15.cloned.1.call-start = ((), (), s32[]{:S(2)}) async-start(), calls=%async_computation.11 | async-start | bytes 2621440 | tf_op jit(solution)/shard_map/all_gather | solution.py:61
  469.5 149.7 %reduce-scatter.11.cloned.1.call-start = ((), (), s32[]{:S(2)}) async-start(), calls=%async_computation.7 | async-start | bytes 655360 | tf_op jit(solution)/shard_map/reduce_scatter | solution.py:70
  513.6 47.4 %collective-permute-start.13 = (bf16[8,1,4,256,128]{4,3,2,1,0:T(8,128)(2,1)}, bf16[8,1,4,256,128]{4,3,2,1,0:T(8,128)(2,1)}, u32[]{:S(2)}, u32[]{:S(2)}) collective-permute-start(bf16[8,1,4,256,128]{4,3,2,1,0:T(8,128)(2,1)} %bitcast.129), channel_id=1, source_target_pairs={{4,0},{8,4},{12,8},{16,12},{20,16},{24,20},{28,24},{0,28},{5,1},{9... | collective-permute-start | bytes 6291464 | tf_op jit(solution)/shard_map/ppermute | solution.py:16
  515.2 47.5 %collective-permute-start.12 = (bf16[8,1,4,256,128]{4,3,2,1,0:T(8,128)(2,1)}, bf16[8,1,4,256,128]{4,3,2,1,0:T(8,128)(2,1)}, u32[]{:S(2)}, u32[]{:S(2)}) collective-permute-start(bf16[8,1,4,256,128]{4,3,2,1,0:T(8,128)(2,1)} %bitcast.130), channel_id=1, source_target_pairs={{0,4},{4,8},{8,12},{12,16},{16,20},{20,24},{24,28},{28,0},{1,5},{5... | collective-permute-start | bytes 6291464 | tf_op jit(solution)/shard_map/ppermute | solution.py:13
  589.8 8.8 %collective-permute-start.15 = (bf16[4,256,128]{2,0,1:T(4,128)(2,1)S(1)}, bf16[4,256,128]{2,0,1:T(4,128)(2,1)S(1)}, u32[]{:S(2)}, u32[]{:S(2)}) collective-permute-start(bf16[4,256,128]{2,0,1:T(4,128)(2,1)S(1)} %get-tuple-element.7), channel_id=1, source_target_pairs={{28,0},{0,4},{4,8},{8,12},{12,16},{16,20},{20,24},{24,28},{29,1},{... | collective-permute-start | bytes 786440 | tf_op jit(solution)/shard_map/ppermute | solution.py:24
  589.9 8.8 %collective-permute-start.14 = (bf16[4,256,128]{2,0,1:T(4,128)(2,1)S(1)}, bf16[4,256,128]{2,0,1:T(4,128)(2,1)S(1)}, u32[]{:S(2)}, u32[]{:S(2)}) collective-permute-start(bf16[4,256,128]{2,0,1:T(4,128)(2,1)S(1)} %get-tuple-element.6), channel_id=1, source_target_pairs={{4,0},{8,4},{12,8},{16,12},{20,16},{24,20},{28,24},{0,28},{5,1},{9... | collective-permute-start | bytes 786440 | tf_op jit(solution)/shard_map/ppermute | solution.py:24
Sparse Core Ops, SparseCore 0:
  8.9 48.3 all-gather.8
  143.6 19.6 reduce-scatter.4
  165.6 43.8 all-gather.10
  295.8 19.5 reduce-scatter.6
  317.7 43.9 all-gather.12
  448.0 19.4 reduce-scatter.8
  469.7 43.8 all-gather.14
  599.9 19.3 reduce-scatter.10
where the time goes:
time: 636 us; the launch traced here: 628 us
  waiting for transfers between devices  430 us (68%)
  matrix products  88.6 us (14%)
  local copies, waits for them, and re-layouts  46.8 us (7%)
  other arithmetic  30.2 us (5%)
  starting transfers between devices  18.5 us (3%)
  between operations  14.2 us (2%)
    all_gather x4, waiting for transfers between devices, on_device(): stacked = lax.all_gather(recent[:, None, None], 'cuts', axis=2, tiled=True)  180 us
    ppermute x4, waiting for transfers between devices, padded(): lax.ppermute(lax.slice_in_dim(block, 0, width, axis=dim), axis, backward)  139 us
    reduce_scatter x4, waiting for transfers between devices, on_device(): lax.psum_scatter(grouped[1] + from_above + from_below, 'cuts', scatter_di...  78.4 us
    dot_general x4, matrix products, near_field(): jnp.einsum('plij,lpjr->ir', lag_kernels, partner_hist, preferred_element_...  48.4 us
    dot_general x4, matrix products, near_field(): jnp.einsum('plij,plir->pjr', lag_kernels, own_hist, preferred_element_typ...  30.4 us
    gather x4, local copies, waits for them, and re-layouts, near_field(): partner_hist = jnp.take(window, pair_partner, axis=1)  27.7 us
    concatenate x4, other arithmetic, padded(): block = jnp.concatenate([low, block, high], axis=dim)  25.8 us
    ppermute x8, waiting for transfers between devices, shifted(): return lax.ppermute(block, axis, route)  24.6 us
  transfers between devices with their start and end apart: 24, of which 20 were waited for; matrix products, arithmetic and copies ran while one was open for 7% of the time, Pallas kernels for 0%

commit v1 on v0

--- a/solution.py
+++ b/solution.py
@@ -58,7 +58,12 @@
     window = history
     outputs = []
     for step_now in range(step_total):
-        stacked = lax.all_gather(recent[:, None, None], "cuts", axis=2, tiled=True)
+        stacked = jnp.concatenate(
+            lax.all_to_all(
+                jnp.stack([recent[:, None, None]] * lax.axis_size("cuts")), "cuts", 0, 0
+            ),
+            axis=2,
+        )
         bordered = padded(stacked, (("region", 1),), 1)
         window = bordered.reshape(lag_total, 3 * cut_count, panel_count, column_count)
         partial_field = near_field(

time: 636 us -> 663 us (1.042)
  blocking collectives: 0 us -> 150 us
  waiting for transfers between devices: 430 us -> 305 us
  other arithmetic: 30.2 us -> 16.7 us
  local copies, waits for them, and re-layouts: 46.8 us -> 59 us
    all_gather x4 -> x0, waiting for transfers between devices: 180 us -> none  [on_device(): stacked = lax.all_gather(recent[:, None, None], 'cuts', axis=2, tiled=True)]
    all_to_all x0 -> x3, blocking collectives: none -> 150 us  [on_device(): lax.all_to_all(jnp.stack([recent[:, None, None]] * lax.axis_size('cuts'))...]
    all_to_all x0 -> x1, waiting for transfers between devices: none -> 48 us  [on_device(): lax.all_to_all(jnp.stack([recent[:, None, None]] * lax.axis_size('cuts'))...]
    concatenate x0 -> x4, local copies, waits for them, and re-layouts: none -> 12.2 us  [padded(): block = jnp.concatenate([low, block, high], axis=dim)]
    concatenate x4, other arithmetic: 25.8 us -> 15.3 us  [padded(): block = jnp.concatenate([low, block, high], axis=dim)]
  transfers between devices with their start and end apart: 24 -> 21, of which waited for: 20 -> 17; matrix products, arithmetic and copies ran while one was open for 7% -> 6% of each run, Pallas kernels for 0% -> 0%
where the time goes in v1:
time: 663 us; the launch traced here: 654 us
  waiting for transfers between devices  305 us (46%)
  blocking collectives  150 us (23%)
  matrix products  88.5 us (13%)
  local copies, waits for them, and re-layouts  59 us (9%)
  starting transfers between devices  20.7 us (3%)
  other arithmetic  16.7 us (3%)
  between operations  13.8 us (2%)
    all_to_all x3, blocking collectives, on_device(): lax.all_to_all(jnp.stack([recent[:, None, None]] * lax.axis_size('cuts'))...  150 us
    ppermute x4, waiting for transfers between devices, padded(): lax.ppermute(lax.slice_in_dim(block, 0, width, axis=dim), axis, backward)  142 us
    reduce_scatter x4, waiting for transfers between devices, on_device(): lax.psum_scatter(grouped[1] + from_above + from_below, 'cuts', scatter_di...  76.7 us
    dot_general x4, matrix products, near_field(): jnp.einsum('plij,lpjr->ir', lag_kernels, partner_hist, preferred_element_...  48.3 us
    all_to_all x1, waiting for transfers between devices, on_device(): lax.all_to_all(jnp.stack([recent[:, None, None]] * lax.axis_size('cuts'))...  48 us
    dot_general x4, matrix products, near_field(): jnp.einsum('plij,plir->pjr', lag_kernels, own_hist, preferred_element_typ...  30.4 us
    gather x4, local copies, waits for them, and re-layouts, near_field(): partner_hist = jnp.take(window, pair_partner, axis=1)  27.5 us
    ppermute x8, waiting for transfers between devices, shifted(): return lax.ppermute(block, axis, route)  27.2 us
  transfers between devices with their start and end apart: 21, of which 17 were waited for; matrix products, arithmetic and copies ran while one was open for 6% of the time, Pallas kernels for 0%

profile of v1, /device:TPU:0, one launch (start us, length us, event | category | flops | bytes accessed | tf_op | source)
XLA Modules:
  0.0 654.5 jit_solution(7967869070600802200)
XLA Ops:
  6.5 2.9 stack.27
  9.5 6.3 all-to-all-start
  16.1 48.0 %all-to-all-done = bf16[4,8,1,1,256,128]{5,4,1,3,2,0:T(8,128)(2,1)} async-done(((bf16[4,8,1,1,256,128]{5,4,1,3,2,0:T(8,128)(2,1)}), bf16[4,8,1,1,256,128]{5,4,1,3,2,0:T(8,128)(2,1)}, u32[]{:S(2)}, u32[]{:S(2)}) %all-to-all-start) | async-done | bytes 2097184 | tf_op jit(solution)/shard_map/all_to_all | solution.py:62
  65.3 7.6 %fusion.28 = f32[12,256,128]{1,2,0:T(8,128)} fusion(bf16[12,8,256,256]{3,2,1,0:T(8,128)(2,1)} %param.11, bf16[8,256,128]{1,2,0:T(8,128)(2,1)S(1)} %copy.43, bf16[12,8]{1,0:T(8,128)(2,1)S(1)} %compare_convert_fusion.1), kind=kOutput, calls=%fused_computation.44 | convolution fusion | flops 1613758464 | bytes 14680256 | tf_op jit(solution)/shard_map/plij,plir->pjr/dot_general | solution.py:39
  72.9 2.1 copy.44
  75.2 36.2 %collective-permute-done.1 = bf16[8,1,4,256,128]{4,3,0,2,1:T(8,128)(2,1)} collective-permute-done((bf16[8,1,4,256,128]{4,3,0,2,1:T(8,128)(2,1)}, bf16[8,1,4,256,128]{4,3,0,2,1:T(8,128)(2,1)}, u32[]{:S(2)}, u32[]{:S(2)}) %collective-permute-start.1) | collective-permute-done | bytes 2097184 | tf_op jit(solution)/shard_map/ppermute | solution.py:16
  113.4 3.8 pad_maximum_fusion
  117.2 3.1 copy.45
  120.3 6.9 %gather_fusion = bf16[12,8,256,128]{3,2,1,0:T(8,128)(2,1)} fusion(bf16[8,12,256,128]{3,2,1,0:T(8,128)(2,1)} %bitcast.131, s32[1024]{0:T(1024)S(1)} %pad_clamp_fusion), kind=kCustom, calls=%fused_computation.clone | custom fusion | bytes 12582960 | tf_op jit(solution)/shard_map/jit(_take)/gather | solution.py:33
  127.1 12.1 %fusion.40 = f32[256,128]{0,1:T(8,128)S(1)} fusion(bf16[12,8,256,256]{3,2,1,0:T(8,128)(2,1)} %param.11, bf16[12,8,256,128]{3,2,1,0:T(8,128)(2,1)} %gather_fusion, pred[12]{0:T(512)(128)(4,1)S(1)} %compare_and_fusion, bf16[8,12]{0,1:T(8,128)(2,1)S(1)} %compare_convert_fusion), kind=kOutput, calls=%fused_computation.48 | convolution fusion | flops 1616904192 | bytes 19005644 | tf_op jit(solution)/shard_map/plij,lpjr->ir/dot_general | solution.py:35
  140.9 2.6 collective-permute-start.2
  143.6 6.7 %collective-permute-done.3 = bf16[4,256,128]{2,0,1:T(4,128)(2,1)S(1)} collective-permute-done((bf16[4,256,128]{2,0,1:T(4,128)(2,1)S(1)}, bf16[4,256,128]{2,0,1:T(4,128)(2,1)S(1)}, u32[]{:S(2)}, u32[]{:S(2)}) %collective-permute-start.3) | collective-permute-done | bytes 262176 | tf_op jit(solution)/shard_map/ppermute | solution.py:24
  151.5 19.2 %reduce-scatter.5.cloned.1.call-done = f32[1,256,128]{2,1,0:T(8,128)} async-done(((f32[4,256,128]{2,1,0:T(8,128)}), f32[1,256,128]{2,1,0:T(8,128)}) %reduce-scatter.5.cloned.1.call-update) | async-done | bytes 131088 | tf_op jit(solution)/shard_map/reduce_scatter | solution.py:75
  172.5 50.1 %all_to_all.20 = bf16[4,8,1,1,256,128]{5,4,1,3,2,0:T(8,128)(2,1)} all-to-all(bf16[4,8,1,1,256,128]{5,4,1,3,2,0:T(8,128)(2,1)S(1)} %stack.29), channel_id=1, replica_groups=mesh['region'=8,'cuts'=4] {'cuts'}, dimensions={0} | all-to-all | bytes 4194304 | tf_op jit(solution)/shard_map/all_to_all | solution.py:62
  223.7 7.6 %fusion.31 = f32[12,256,128]{1,2,0:T(8,128)} fusion(bf16[12,8,256,256]{3,2,1,0:T(8,128)(2,1)} %param.11, bf16[8,256,128]{1,2,0:T(8,128)(2,1)S(1)} %copy.51, bf16[12,8]{1,0:T(8,128)(2,1)S(1)} %compare_convert_fusion.1), kind=kOutput, calls=%fused_computation.45 | convolution fusion | flops 1613758464 | bytes 14680256 | tf_op jit(solution)/shard_map/plij,plir->pjr/dot_general | solution.py:39
  231.3 2.1 copy.52
  233.5 35.0 %collective-permute-done.5 = bf16[8,1,4,256,128]{4,3,0,2,1:T(8,128)(2,1)} collective-permute-done((bf16[8,1,4,256,128]{4,3,0,2,1:T(8,128)(2,1)}, bf16[8,1,4,256,128]{4,3,0,2,1:T(8,128)(2,1)}, u32[]{:S(2)}, u32[]{:S(2)}) %collective-permute-start.5) | collective-permute-done | bytes 2097184 | tf_op jit(solution)/shard_map/ppermute | solution.py:16
  268.5 3.2 collective-permute-done.4
  271.7 3.8 pad_maximum_fusion.1
  275.5 3.1 copy.53
  278.6 6.9 %gather_fusion.1 = bf16[12,8,256,128]{3,2,1,0:T(8,128)(2,1)} fusion(bf16[8,12,256,128]{3,2,1,0:T(8,128)(2,1)} %bitcast.132, s32[1024]{0:T(1024)S(1)} %pad_clamp_fusion), kind=kCustom, calls=%fused_computation.1.clone | custom fusion | bytes 12582960 | tf_op jit(solution)/shard_map/jit(_take)/gather | solution.py:33
  285.5 12.1 %fusion.45 = f32[256,128]{0,1:T(8,128)S(1)} fusion(bf16[12,8,256,256]{3,2,1,0:T(8,128)(2,1)} %param.11, bf16[12,8,256,128]{3,2,1,0:T(8,128)(2,1)} %gather_fusion.1, pred[12]{0:T(512)(128)(4,1)S(1)} %copy-done.9, bf16[8,12]{0,1:T(8,128)(2,1)S(1)} %copy-done.5), kind=kOutput, calls=%fused_computation.49 | convolution fusion | flops 1616904192 | bytes 19005644 | tf_op jit(solution)/shard_map/plij,lpjr->ir/dot_general | solution.py:35
  299.3 2.6 collective-permute-start.6
  301.9 6.8 %collective-permute-done.7 = bf16[4,256,128]{2,0,1:T(4,128)(2,1)S(1)} collective-permute-done((bf16[4,256,128]{2,0,1:T(4,128)(2,1)S(1)}, bf16[4,256,128]{2,0,1:T(4,128)(2,1)S(1)}, u32[]{:S(2)}, u32[]{:S(2)}) %collective-permute-start.7) | collective-permute-done | bytes 262176 | tf_op jit(solution)/shard_map/ppermute | solution.py:24
  309.9 19.1 %reduce-scatter.7.cloned.1.call-done = f32[1,256,128]{2,1,0:T(8,128)} async-done(((f32[4,256,128]{2,1,0:T(8,128)}), f32[1,256,128]{2,1,0:T(8,128)}) %reduce-scatter.7.cloned.1.call-update) | async-done | bytes 131088 | tf_op jit(solution)/shard_map/reduce_scatter | solution.py:75
  330.8 50.1 %all_to_all.21 = bf16[4,8,1,1,256,128]{5,4,1,3,2,0:T(8,128)(2,1)} all-to-all(bf16[4,8,1,1,256,128]{5,4,1,3,2,0:T(8,128)(2,1)S(1)} %stack.31), channel_id=1, replica_groups=mesh['region'=8,'cuts'=4] {'cuts'}, dimensions={0} | all-to-all | bytes 4194304 | tf_op jit(solution)/shard_map/all_to_all | solution.py:62
  381.8 7.6 %fusion.34 = f32[12,256,128]{1,2,0:T(8,128)} fusion(bf16[12,8,256,256]{3,2,1,0:T(8,128)(2,1)} %param.11, bf16[8,256,128]{1,2,0:T(8,128)(2,1)S(1)} %copy.59, bf16[12,8]{1,0:T(8,128)(2,1)S(1)} %compare_convert_fusion.1), kind=kOutput, calls=%fused_computation.46 | convolution fusion | flops 1613758464 | bytes 14680256 | tf_op jit(solution)/shard_map/plij,plir->pjr/dot_general | solution.py:39
  389.4 2.1 copy.60
  391.5 35.7 %collective-permute-done.9 = bf16[8,1,4,256,128]{4,3,0,2,1:T(8,128)(2,1)} collective-permute-done((bf16[8,1,4,256,128]{4,3,0,2,1:T(8,128)(2,1)}, bf16[8,1,4,256,128]{4,3,0,2,1:T(8,128)(2,1)}, u32[]{:S(2)}, u32[]{:S(2)}) %collective-permute-start.9) | collective-permute-done | bytes 2097184 | tf_op jit(solution)/shard_map/ppermute | solution.py:16
  427.2 2.9 collective-permute-done.8
  430.1 3.8 pad_maximum_fusion.2
  433.9 3.0 copy.61
  437.0 6.9 %gather_fusion.2 = bf16[12,8,256,128]{3,2,1,0:T(8,128)(2,1)} fusion(bf16[8,12,256,128]{3,2,1,0:T(8,128)(2,1)} %bitcast.133, s32[1024]{0:T(1024)S(1)} %pad_clamp_fusion), kind=kCustom, calls=%fused_computation.2.clone | custom fusion | bytes 12582960 | tf_op jit(solution)/shard_map/jit(_take)/gather | solution.py:33
  443.9 12.1 %fusion.50 = f32[256,128]{0,1:T(8,128)S(1)} fusion(bf16[12,8,256,256]{3,2,1,0:T(8,128)(2,1)} %param.11, bf16[12,8,256,128]{3,2,1,0:T(8,128)(2,1)} %gather_fusion.2, pred[12]{0:T(512)(128)(4,1)S(1)} %copy-done.10, bf16[8,12]{0,1:T(8,128)(2,1)S(1)} %copy-done.6), kind=kOutput, calls=%fused_computation.50 | convolution fusion | flops 1616904192 | bytes 19005644 | tf_op jit(solution)/shard_map/plij,lpjr->ir/dot_general | solution.py:35
  457.6 2.6 collective-permute-start.10
  460.3 6.8 %collective-permute-done.11 = bf16[4,256,128]{2,0,1:T(4,128)(2,1)S(1)} collective-permute-done((bf16[4,256,128]{2,0,1:T(4,128)(2,1)S(1)}, bf16[4,256,128]{2,0,1:T(4,128)(2,1)S(1)}, u32[]{:S(2)}, u32[]{:S(2)}) %collective-permute-start.11) | collective-permute-done | bytes 262176 | tf_op jit(solution)/shard_map/ppermute | solution.py:24
  468.3 19.1 %reduce-scatter.9.cloned.1.call-done = f32[1,256,128]{2,1,0:T(8,128)} async-done(((f32[4,256,128]{2,1,0:T(8,128)}), f32[1,256,128]{2,1,0:T(8,128)}) %reduce-scatter.9.cloned.1.call-update) | async-done | bytes 131088 | tf_op jit(solution)/shard_map/reduce_scatter | solution.py:75
  489.2 50.1 %all_to_all.22 = bf16[4,8,1,1,256,128]{5,4,1,3,2,0:T(8,128)(2,1)} all-to-all(bf16[4,8,1,1,256,128]{5,4,1,3,2,0:T(8,128)(2,1)S(1)} %stack.33), channel_id=1, replica_groups=mesh['region'=8,'cuts'=4] {'cuts'}, dimensions={0} | all-to-all | bytes 4194304 | tf_op jit(solution)/shard_map/all_to_all | solution.py:62
  540.2 7.6 %fusion.37 = f32[12,256,128]{1,2,0:T(8,128)} fusion(bf16[12,8,256,256]{3,2,1,0:T(8,128)(2,1)} %param.11, bf16[8,256,128]{1,2,0:T(8,128)(2,1)S(1)} %copy.67, bf16[12,8]{1,0:T(8,128)(2,1)S(1)} %compare_convert_fusion.1), kind=kOutput, calls=%fused_computation.47 | convolution fusion | flops 1613758464 | bytes 14680256 | tf_op jit(solution)/shard_map/plij,plir->pjr/dot_general | solution.py:39
  549.9 35.5 %collective-permute-done.13 = bf16[8,1,4,256,128]{4,3,0,2,1:T(8,128)(2,1)} collective-permute-done((bf16[8,1,4,256,128]{4,3,0,2,1:T(8,128)(2,1)}, bf16[8,1,4,256,128]{4,3,0,2,1:T(8,128)(2,1)}, u32[]{:S(2)}, u32[]{:S(2)}) %collective-permute-start.13) | collective-permute-done | bytes 2097184 | tf_op jit(solution)/shard_map/ppermute | solution.py:16
  585.5 3.0 collective-permute-done.12
  588.4 3.8 pad_maximum_fusion.3
  592.3 3.1 copy.69
  595.3 6.9 %gather_fusion.3 = bf16[12,8,256,128]{3,2,1,0:T(8,128)(2,1)} fusion(bf16[8,12,256,128]{3,2,1,0:T(8,128)(2,1)} %bitcast.130, s32[1024]{0:T(1024)S(1)} %pad_clamp_fusion), kind=kCustom, calls=%fused_computation.3.clone | custom fusion | bytes 12582960 | tf_op jit(solution)/shard_map/jit(_take)/gather | solution.py:33
  602.2 12.1 %fusion.55 = f32[256,128]{0,1:T(8,128)S(1)} fusion(bf16[12,8,256,256]{3,2,1,0:T(8,128)(2,1)} %param.11, bf16[12,8,256,128]{3,2,1,0:T(8,128)(2,1)} %gather_fusion.3, pred[12]{0:T(512)(128)(4,1)S(1)} %copy-done.10, bf16[8,12]{0,1:T(8,128)(2,1)S(1)} %copy-done.6), kind=kOutput, calls=%fused_computation.51 | convolution fusion | flops 1616904192 | bytes 19005644 | tf_op jit(solution)/shard_map/plij,lpjr->ir/dot_general | solution.py:35
  616.0 2.6 collective-permute-start.14
  618.6 6.8 %collective-permute-done.15 = bf16[4,256,128]{2,0,1:T(4,128)(2,1)S(1)} collective-permute-done((bf16[4,256,128]{2,0,1:T(4,128)(2,1)S(1)}, bf16[4,256,128]{2,0,1:T(4,128)(2,1)S(1)}, u32[]{:S(2)}, u32[]{:S(2)}) %collective-permute-start.15) | collective-permute-done | bytes 262176 | tf_op jit(solution)/shard_map/ppermute | solution.py:24
  626.5 19.2 %reduce-scatter.11.cloned.1.call-done = f32[1,256,128]{2,1,0:T(8,128)} async-done(((f32[4,256,128]{2,1,0:T(8,128)}), f32[1,256,128]{2,1,0:T(8,128)}) %reduce-scatter.11.cloned.1.call-update) | async-done | bytes 131088 | tf_op jit(solution)/shard_map/reduce_scatter | solution.py:75
  (97 shorter events, 27.0 us)
Async XLA Ops:
  6.5 164.2 %copy-start = (bf16[256,256]{1,0:T(8,128)(2,1)S(1)}, bf16[256,256]{1,0:T(8,128)(2,1)}, u32[]{:S(2)}) copy-start(bf16[256,256]{1,0:T(8,128)(2,1)} %param.10) | copy-start | bytes 393220
  6.5 9.3 %copy-start.1 = (bf16[8,256,128]{2,1,0:T(8,128)(2,1)S(1)}, bf16[8,256,128]{2,1,0:T(8,128)(2,1)}, u32[]{:S(2)}) copy-start(bf16[8,256,128]{2,1,0:T(8,128)(2,1)} %param.8) | copy-start | bytes 1572868
  6.5 9.5 %copy-start.7 = (s32[12]{0:T(128)S(1)}, s32[12]{0:T(128)}, u32[]{:S(2)}) copy-start(s32[12]{0:T(128)} %param.13) | copy-start | bytes 148
  9.5 54.6 %all-to-all-start = ((bf16[4,8,1,1,256,128]{5,4,1,3,2,0:T(8,128)(2,1)}), bf16[4,8,1,1,256,128]{5,4,1,3,2,0:T(8,128)(2,1)}, u32[]{:S(2)}, u32[]{:S(2)}) async-start(bf16[4,8,1,1,256,128]{5,4,1,3,2,0:T(8,128)(2,1)} %stack.27), calls=%async_computation | async-start | bytes 4194304 | tf_op jit(solution)/shard_map/all_to_all | solution.py:62
  15.8 154.9 %reduce-scatter.5.cloned.1.call-start = ((), (), s32[]{:S(2)}) async-start(), calls=%async_computation.8 | async-start | bytes 655360 | tf_op jit(solution)/shard_map/reduce_scatter | solution.py:75
  64.1 10.9 %copy-start.3 = (s32[12]{0:T(128)S(1)}, s32[12]{0:T(128)}, u32[]{:S(2)}) copy-start(s32[12]{0:T(128)} %param.12) | copy-start | bytes 148
  64.1 47.3 %collective-permute-start.1 = (bf16[8,1,4,256,128]{4,3,0,2,1:T(8,128)(2,1)}, bf16[8,1,4,256,128]{4,3,0,2,1:T(8,128)(2,1)}, u32[]{:S(2)}, u32[]{:S(2)}) collective-permute-start(bf16[8,1,4,256,128]{4,3,0,2,1:T(8,128)(2,1)} %bitcast.5), channel_id=1, source_target_pairs={{4,0},{8,4},{12,8},{16,12},{20,16},{24,20},{28,24},{0,28},{5,1},{9... | collective-permute-start | bytes 6291464 | tf_op jit(solution)/shard_map/ppermute | solution.py:16
  65.3 48.1 %collective-permute-start = (bf16[8,1,4,256,128]{4,3,0,2,1:T(8,128)(2,1)}, bf16[8,1,4,256,128]{4,3,0,2,1:T(8,128)(2,1)}, u32[]{:S(2)}, u32[]{:S(2)}) collective-permute-start(bf16[8,1,4,256,128]{4,3,0,2,1:T(8,128)(2,1)} %bitcast.5), channel_id=1, source_target_pairs={{0,4},{4,8},{8,12},{12,16},{16,20},{20,24},{24,28},{28,0},{1,5},{5... | collective-permute-start | bytes 6291464 | tf_op jit(solution)/shard_map/ppermute | solution.py:13
  75.1 52.0 %copy-start.8 = (pred[12]{0:T(512)(128)(4,1)}, pred[12]{0:T(512)(128)(4,1)S(1)}, u32[]{:S(2)}) copy-start(pred[12]{0:T(512)(128)(4,1)S(1)} %compare_and_fusion) | copy-start | bytes 40
  75.2 52.0 %copy-start.4 = (bf16[8,12]{0,1:T(8,128)(2,1)}, bf16[8,12]{0,1:T(8,128)(2,1)S(1)}, u32[]{:S(2)}) copy-start(bf16[8,12]{0,1:T(8,128)(2,1)S(1)} %compare_convert_fusion) | copy-start | bytes 580
  139.2 31.5 %copy-start.2 = (bf16[4,256,128]{2,1,0:T(8,128)(2,1)S(1)}, bf16[4,256,128]{2,1,0:T(8,128)(2,1)}, u32[]{:S(2)}) copy-start(bf16[4,256,128]{2,1,0:T(8,128)(2,1)} %param.9) | copy-start | bytes 786436
  140.9 9.4 %collective-permute-start.3 = (bf16[4,256,128]{2,0,1:T(4,128)(2,1)S(1)}, bf16[4,256,128]{2,0,1:T(4,128)(2,1)S(1)}, u32[]{:S(2)}, u32[]{:S(2)}) collective-permute-start(bf16[4,256,128]{2,0,1:T(4,128)(2,1)S(1)} %get-tuple-element.13), channel_id=1, source_target_pairs={{28,0},{0,4},{4,8},{8,12},{12,16},{16,20},{20,24},{24,28},{29,1},{... | collective-permute-start | bytes 786440 | tf_op jit(solution)/shard_map/ppermute | solution.py:24
  140.9 9.4 %collective-permute-start.2 = (bf16[4,256,128]{2,0,1:T(4,128)(2,1)S(1)}, bf16[4,256,128]{2,0,1:T(4,128)(2,1)S(1)}, u32[]{:S(2)}, u32[]{:S(2)}) collective-permute-start(bf16[4,256,128]{2,0,1:T(4,128)(2,1)S(1)} %get-tuple-element.12), channel_id=1, source_target_pairs={{4,0},{8,4},{12,8},{16,12},{20,16},{24,20},{28,24},{0,28},{5,1},{9... | collective-permute-start | bytes 786440 | tf_op jit(solution)/shard_map/ppermute | solution.py:24
  151.4 177.7 %reduce-scatter.7.cloned.1.call-start = ((), (), s32[]{:S(2)}) async-start(), calls=%async_computation.9 | async-start | bytes 655360 | tf_op jit(solution)/shard_map/reduce_scatter | solution.py:75
  222.5 45.9 %collective-permute-start.5 = (bf16[8,1,4,256,128]{4,3,0,2,1:T(8,128)(2,1)}, bf16[8,1,4,256,128]{4,3,0,2,1:T(8,128)(2,1)}, u32[]{:S(2)}, u32[]{:S(2)}) collective-permute-start(bf16[8,1,4,256,128]{4,3,0,2,1:T(8,128)(2,1)} %bitcast.20), channel_id=1, source_target_pairs={{4,0},{8,4},{12,8},{16,12},{20,16},{24,20},{28,24},{0,28},{5,1},{9... | collective-permute-start | bytes 6291464 | tf_op jit(solution)/shard_map/ppermute | solution.py:16
  223.0 48.7 %collective-permute-start.4 = (bf16[8,1,4,256,128]{4,3,0,2,1:T(8,128)(2,1)}, bf16[8,1,4,256,128]{4,3,0,2,1:T(8,128)(2,1)}, u32[]{:S(2)}, u32[]{:S(2)}) collective-permute-start(bf16[8,1,4,256,128]{4,3,0,2,1:T(8,128)(2,1)} %bitcast.20), channel_id=1, source_target_pairs={{0,4},{4,8},{8,12},{12,16},{16,20},{20,24},{24,28},{28,0},{1,5},{5... | collective-permute-start | bytes 6291464 | tf_op jit(solution)/shard_map/ppermute | solution.py:13
  278.6 6.9 %copy-start.5 = (bf16[8,12]{0,1:T(8,128)(2,1)S(1)}, bf16[8,12]{0,1:T(8,128)(2,1)}, u32[]{:S(2)}) copy-start(bf16[8,12]{0,1:T(8,128)(2,1)} %copy-done.4) | copy-start | bytes 580
  278.6 6.9 %copy-start.9 = (pred[12]{0:T(512)(128)(4,1)S(1)}, pred[12]{0:T(512)(128)(4,1)}, u32[]{:S(2)}) copy-start(pred[12]{0:T(512)(128)(4,1)} %copy-done.8) | copy-start | bytes 40
  299.2 9.5 %collective-permute-start.7 = (bf16[4,256,128]{2,0,1:T(4,128)(2,1)S(1)}, bf16[4,256,128]{2,0,1:T(4,128)(2,1)S(1)}, u32[]{:S(2)}, u32[]{:S(2)}) collective-permute-start(bf16[4,256,128]{2,0,1:T(4,128)(2,1)S(1)} %get-tuple-element.11), channel_id=1, source_target_pairs={{28,0},{0,4},{4,8},{8,12},{12,16},{16,20},{20,24},{24,28},{29,1},{... | collective-permute-start | bytes 786440 | tf_op jit(solution)/shard_map/ppermute | solution.py:24
  299.3 9.5 %collective-permute-start.6 = (bf16[4,256,128]{2,0,1:T(4,128)(2,1)S(1)}, bf16[4,256,128]{2,0,1:T(4,128)(2,1)S(1)}, u32[]{:S(2)}, u32[]{:S(2)}) collective-permute-start(bf16[4,256,128]{2,0,1:T(4,128)(2,1)S(1)} %get-tuple-element.10), channel_id=1, source_target_pairs={{4,0},{8,4},{12,8},{16,12},{20,16},{24,20},{28,24},{0,28},{5,1},{9... | collective-permute-start | bytes 786440 | tf_op jit(solution)/shard_map/ppermute | solution.py:24
  309.8 177.6 %reduce-scatter.9.cloned.1.call-start = ((), (), s32[]{:S(2)}) async-start(), calls=%async_computation.10 | async-start | bytes 655360 | tf_op jit(solution)/shard_map/reduce_scatter | solution.py:75
  380.9 46.3 %collective-permute-start.9 = (bf16[8,1,4,256,128]{4,3,0,2,1:T(8,128)(2,1)}, bf16[8,1,4,256,128]{4,3,0,2,1:T(8,128)(2,1)}, u32[]{:S(2)}, u32[]{:S(2)}) collective-permute-start(bf16[8,1,4,256,128]{4,3,0,2,1:T(8,128)(2,1)} %bitcast.35), channel_id=1, source_target_pairs={{4,0},{8,4},{12,8},{16,12},{20,16},{24,20},{28,24},{0,28},{5,1},{9... | collective-permute-start | bytes 6291464 | tf_op jit(solution)/shard_map/ppermute | solution.py:16
  381.4 48.7 %collective-permute-start.8 = (bf16[8,1,4,256,128]{4,3,0,2,1:T(8,128)(2,1)}, bf16[8,1,4,256,128]{4,3,0,2,1:T(8,128)(2,1)}, u32[]{:S(2)}, u32[]{:S(2)}) collective-permute-start(bf16[8,1,4,256,128]{4,3,0,2,1:T(8,128)(2,1)} %bitcast.35), channel_id=1, source_target_pairs={{0,4},{4,8},{8,12},{12,16},{16,20},{20,24},{24,28},{28,0},{1,5},{5... | collective-permute-start | bytes 6291464 | tf_op jit(solution)/shard_map/ppermute | solution.py:13
  437.0 6.9 %copy-start.6 = (bf16[8,12]{0,1:T(8,128)(2,1)S(1)}, bf16[8,12]{0,1:T(8,128)(2,1)}, u32[]{:S(2)}) copy-start(bf16[8,12]{0,1:T(8,128)(2,1)} %copy-done.4) | copy-start | bytes 580
  437.0 6.9 %copy-start.10 = (pred[12]{0:T(512)(128)(4,1)S(1)}, pred[12]{0:T(512)(128)(4,1)}, u32[]{:S(2)}) copy-start(pred[12]{0:T(512)(128)(4,1)} %copy-done.8) | copy-start | bytes 40
  457.6 9.5 %collective-permute-start.11 = (bf16[4,256,128]{2,0,1:T(4,128)(2,1)S(1)}, bf16[4,256,128]{2,0,1:T(4,128)(2,1)S(1)}, u32[]{:S(2)}, u32[]{:S(2)}) collective-permute-start(bf16[4,256,128]{2,0,1:T(4,128)(2,1)S(1)} %get-tuple-element.9), channel_id=1, source_target_pairs={{28,0},{0,4},{4,8},{8,12},{12,16},{16,20},{20,24},{24,28},{29,1},{... | collective-permute-start | bytes 786440 | tf_op jit(solution)/shard_map/ppermute | solution.py:24
  457.6 9.4 %collective-permute-start.10 = (bf16[4,256,128]{2,0,1:T(4,128)(2,1)S(1)}, bf16[4,256,128]{2,0,1:T(4,128)(2,1)S(1)}, u32[]{:S(2)}, u32[]{:S(2)}) collective-permute-start(bf16[4,256,128]{2,0,1:T(4,128)(2,1)S(1)} %get-tuple-element.8), channel_id=1, source_target_pairs={{4,0},{8,4},{12,8},{16,12},{20,16},{24,20},{28,24},{0,28},{5,1},{9... | collective-permute-start | bytes 786440 | tf_op jit(solution)/shard_map/ppermute | solution.py:24
  468.2 177.5 %reduce-scatter.11.cloned.1.call-start = ((), (), s32[]{:S(2)}) async-start(), calls=%async_computation.11 | async-start | bytes 655360 | tf_op jit(solution)/shard_map/reduce_scatter | solution.py:75
  539.2 46.2 %collective-permute-start.13 = (bf16[8,1,4,256,128]{4,3,0,2,1:T(8,128)(2,1)}, bf16[8,1,4,256,128]{4,3,0,2,1:T(8,128)(2,1)}, u32[]{:S(2)}, u32[]{:S(2)}) collective-permute-start(bf16[8,1,4,256,128]{4,3,0,2,1:T(8,128)(2,1)} %bitcast.50), channel_id=1, source_target_pairs={{4,0},{8,4},{12,8},{16,12},{20,16},{24,20},{28,24},{0,28},{5,1},{9... | collective-permute-start | bytes 6291464 | tf_op jit(solution)/shard_map/ppermute | solution.py:16
  539.7 48.7 %collective-permute-start.12 = (bf16[8,1,4,256,128]{4,3,0,2,1:T(8,128)(2,1)}, bf16[8,1,4,256,128]{4,3,0,2,1:T(8,128)(2,1)}, u32[]{:S(2)}, u32[]{:S(2)}) collective-permute-start(bf16[8,1,4,256,128]{4,3,0,2,1:T(8,128)(2,1)} %bitcast.50), channel_id=1, source_target_pairs={{0,4},{4,8},{8,12},{12,16},{16,20},{20,24},{24,28},{28,0},{1,5},{5... | collective-permute-start | bytes 6291464 | tf_op jit(solution)/shard_map/ppermute | solution.py:13
  615.9 9.5 %collective-permute-start.15 = (bf16[4,256,128]{2,0,1:T(4,128)(2,1)S(1)}, bf16[4,256,128]{2,0,1:T(4,128)(2,1)S(1)}, u32[]{:S(2)}, u32[]{:S(2)}) collective-permute-start(bf16[4,256,128]{2,0,1:T(4,128)(2,1)S(1)} %get-tuple-element.7), channel_id=1, source_target_pairs={{28,0},{0,4},{4,8},{8,12},{12,16},{16,20},{20,24},{24,28},{29,1},{... | collective-permute-start | bytes 786440 | tf_op jit(solution)/shard_map/ppermute | solution.py:24
  616.0 9.5 %collective-permute-start.14 = (bf16[4,256,128]{2,0,1:T(4,128)(2,1)S(1)}, bf16[4,256,128]{2,0,1:T(4,128)(2,1)S(1)}, u32[]{:S(2)}, u32[]{:S(2)}) collective-permute-start(bf16[4,256,128]{2,0,1:T(4,128)(2,1)S(1)} %get-tuple-element.6), channel_id=1, source_target_pairs={{4,0},{8,4},{12,8},{16,12},{20,16},{24,20},{28,24},{0,28},{5,1},{9... | collective-permute-start | bytes 786440 | tf_op jit(solution)/shard_map/ppermute | solution.py:24
Sparse Core Ops, SparseCore 0:
  151.5 19.1 reduce-scatter.4
  309.9 19.0 reduce-scatter.6
  468.3 19.0 reduce-scatter.8
  626.6 19.0 reduce-scatter.10
